TPU v7x, 32 devices: a whole 2x2x4 slice. The times are simulated.
32 devices in a mesh: row: 4 (over y, x), col: 8 (over z, core).
Axes of the slice: x: 2, y: 2, z: 4, core: 2. Of those that a mesh axis runs over, the one named last changes fastest.
Arguments:
- throat_owner: int32 [16384, 1], P(('row', 'col')), may hold values from 0 to 3; in each aligned block of 512 rows (0 to 511, 512 to 1023, ...) at most 128 rows name the same one
- throat_interior: int32 [16384], P(('row', 'col')), may hold values from 0 to 895
- throat_offset: int32 [16384], P(('row', 'col')), may hold values from 0 to 4095
- throat_conductance: float32 [16384], P(('row', 'col')), may hold values from 0.1 to 1
- child_update: bfloat16 [7168, 16384], P('col', 'row'), may hold values from -0.09375 to 0.09375
- panel_pores: int32 [4096], replicated, may hold values from 0 to 16383, as said below
- interior_inverse: bfloat16 [7168, 896], P('col'), as said below
- separator_rows: float32 [4096, 16384], P('col', 'row'), may hold values from -6 to 6
Outputs:
- schur_rows: float32 [4096, 16384], P('col', 'row')
Inputs may be any that keep to these rules, and one draw needn't show every extreme that they name: `throat_owner`: in each device's block of 512 throats no owner is named more than 128 times, a bound that some block reaches. `panel_pores`: the 4096 pores are distinct; at most 1536 of them lie in any one owner's range of 4096 pores, and one owner holds exactly 1536. `interior_inverse`: each group's block of 896 rows is lower triangular with diagonal entries between 0.8 and 1.2.
All inputs are finite; a program needn't handle non-finite values.
Results may differ from a plain program's by a relative error of at most 0.01.
Values may be sent and summed in bfloat16 or wider, within the bound.
No kernel may reach another device: no remote copies, remote signals or barrier semaphores. Data moves between devices by JAX's collectives and lax.ppermute only.
A program may use at most 128 MiB of HBM per device.

v0:
```python
import jax
import jax.numpy as jnp
from jax import lax
from jax.sharding import PartitionSpec as P


def rank_within(owners, owner_count):
    onehot = (owners[:, None] == jnp.arange(owner_count, dtype=jnp.int32)[None, :]).astype(
        jnp.int32
    )
    before = jnp.cumsum(onehot, axis=0) - onehot
    return jnp.sum(before * onehot, axis=1)


def panel_slots(panel_pores, owner_width, row_count, row_index):
    panel_total = panel_pores.shape[0]
    panel_owner = panel_pores // owner_width
    panel_within = rank_within(panel_owner, row_count)
    panel_limit = 3 * panel_total // (2 * row_count)
    picked = jnp.where(panel_owner == row_index, panel_within, panel_limit)
    chosen = (
        jnp.zeros((panel_limit,), jnp.int32)
        .at[picked]
        .set(panel_pores - panel_owner * owner_width, mode="drop")
    )
    placed = panel_owner * panel_limit + panel_within
    return (chosen, placed)


def per_device(
    throat_owner,
    throat_interior,
    throat_offset,
    throat_conductance,
    child_update,
    panel_pores,
    interior_inverse,
    separator_rows,
):
    row_count = lax.axis_size("row")
    row_index = lax.axis_index("row")
    owner_width = separator_rows.shape[1]
    throats = throat_interior.shape[0]
    slot_limit = throats // 4
    owners = throat_owner[:, 0]
    slot_ids = owners * slot_limit + rank_within(owners, row_count)
    total_slots = row_count * slot_limit
    rows_sent = jnp.zeros((total_slots,), jnp.int32).at[slot_ids].set(throat_interior)
    cols_sent = jnp.zeros((total_slots,), jnp.int32).at[slot_ids].set(throat_offset)
    values_sent = jnp.zeros((total_slots,), jnp.float32).at[slot_ids].set(throat_conductance)
    index_block = jnp.stack(
        [rows_sent.reshape(row_count, slot_limit), cols_sent.reshape(row_count, slot_limit)], axis=1
    )
    index_back, values_back = (
        lax.all_to_all(index_block, "row", split_axis=0, concat_axis=0, tiled=True),
        lax.all_to_all(
            values_sent.reshape(row_count, slot_limit),
            "row",
            split_axis=0,
            concat_axis=0,
            tiled=True,
        ),
    )
    summed = (
        child_update.astype(jnp.float32)
        .at[index_back[:, 0, :].ravel(), index_back[:, 1, :].ravel()]
        .add(values_back.ravel())
    )
    coupling = summed.astype(jnp.bfloat16)
    solved = jnp.dot(interior_inverse, coupling, preferred_element_type=jnp.float32).astype(
        jnp.bfloat16
    )
    chosen, placed = panel_slots(panel_pores, owner_width, row_count, row_index)
    local_columns = jnp.take(solved, chosen, axis=1)
    gathered = lax.all_gather(local_columns, "row", axis=1, tiled=True)
    panel_solved = jnp.take(gathered, placed, axis=1)
    update = lax.psum_scatter(
        jnp.dot(panel_solved.T, solved, preferred_element_type=jnp.float32).astype(jnp.bfloat16),
        "col",
        scatter_dimension=0,
        tiled=True,
    ).astype(jnp.float32)
    return separator_rows - update


def solution(mesh):
    in_specs = (
        P(("row", "col"), None),
        P(("row", "col")),
        P(("row", "col")),
        P(("row", "col")),
        P("col", "row"),
        P(),
        P("col", None),
        P("col", "row"),
    )
    out_specs = P("col", "row")
    return jax.shard_map(
        per_device, mesh=mesh, in_specs=in_specs, out_specs=out_specs, check_vma=False
    )
```

profile of v0, /device:TPU:0, one launch (start us, length us, event | category | flops | bytes accessed | tf_op | source)
XLA Modules:
  0.0 674.5 jit_solution(6133341720263990972)
XLA Ops:
  6.5 0.0 copy-start
  6.5 0.8 fusion.17
  7.3 1.2 reduce-window.16
  8.6 0.2 slice_reduce_fusion.1
  8.8 0.2 reduce-window.19
  8.9 0.1 add_bitcast_fusion.1
  9.0 0.7 fusion.16
  9.7 0.7 compare_select_fusion.5
  10.4 2.6 scatter_custom_fusion.2
  13.0 2.6 scatter_custom_fusion.1
  15.6 0.6 pad_add_fusion
  16.2 5.2 all-to-all-start
  21.4 0.7 add_select_fusion
  22.1 1.2 reduce-window.14
  23.3 0.2 slice_reduce_fusion
  23.5 0.2 reduce-window.15
  23.7 0.1 add_bitcast_fusion
  23.8 0.1 fusion.10
  23.9 0.7 broadcast_clamp_fusion
  24.7 15.5 %scatter_custom_fusion = s32[1536]{0:T(1024)S(1)} fusion(s32[4096]{0:T(1024)S(1)} %get-tuple-element.6, s32[4096]{0:T(1024)S(1)} %get-tuple-element.7, s32[]{:T(128)} %constant.39.clone.1), kind=kCustom, calls=%fused_computation.54 | custom fusion | bytes 6148 | tf_op jit(solution)/shard_map/scatter | solution.py:24
  40.2 10.3 %convert_element_type.34 = f32[896,4096]{1,0:T(8,128)} convert(bf16[896,4096]{1,0:T(8,128)(2,1)} %param.12) | non-fusion elementwise | flops 3670016 | bytes 22020096 | tf_op jit(solution)/shard_map/convert_element_type | solution.py:65
  50.5 3.2 scatter_custom_fusion.3
  53.7 0.0 all-to-all-done
  53.7 4.2 all-to-all-start.1
  57.9 0.0 all-gather.2.cloned.1.call-start
  57.9 4.5 all-to-all-done.1
  62.4 61.5 %scatter_fusion = f32[896,4096]{1,0:T(8,128)} fusion(f32[896,4096]{1,0:T(8,128)} %convert_element_type.34, s32[512]{0:T(512)S(1)} %bitcast.67, f32[512]{0:T(512)S(1)} %bitcast.70), kind=kCustom, calls=%fused_computation.6 | custom fusion | flops 512 | bytes 10240 | tf_op jit(solution)/shard_map/scatter-add | solution.py:67
  123.8 0.0 copy-done
  123.8 16.1 %fusion.4 = bf16[4096,896]{1,0:T(8,128)(2,1)} fusion(bf16[896,896]{1,0:T(8,128)(2,1)S(1)} %copy-done, f32[896,4096]{1,0:T(8,128)} %scatter_fusion), kind=kOutput, calls=%fused_computation.13 | convolution fusion | flops 6584008704 | bytes 23625728 | tf_op jit(solution)/shard_map/dot_general | solution.py:70
  139.9 11.1 %gather_fusion = bf16[1536,896]{1,0:T(8,128)(2,1)} fusion(bf16[896,4096]{0,1:T(8,128)(2,1)} %bitcast.66, s32[2048]{0:T(1024)S(1)} %pad_clamp_fusion), kind=kCustom, calls=%fused_computation | custom fusion | bytes 5511168 | tf_op jit(solution)/shard_map/jit(_take)/gather | solution.py:74
  151.0 0.0 copy-start.2
  151.0 3.8 select_bitcast_fusion
  154.8 0.0 all-gather.2.cloned.1.call-update
  154.9 0.3 reduce-scatter.2.cloned.1.call-start
  155.1 0.0 copy-done.2
  155.2 108.6 %all-gather.2.cloned.1.call-done = bf16[896,6144]{0,1:T(8,128)(2,1)} async-done(((bf16[896,1536]{0,1:T(8,128)(2,1)}), bf16[896,6144]{0,1:T(8,128)(2,1)}) %all-gather.2.cloned.1.call-update) | async-done | bytes 11010064 | tf_op jit(solution)/shard_map/all_gather | solution.py:75
  263.8 25.3 %gather_fusion.1 = bf16[4096,896]{1,0:T(8,128)(2,1)} fusion(bf16[896,6144]{0,1:T(8,128)(2,1)} %all-gather.2.cloned.1.call-done, s32[4096]{0:T(1024)S(1)} %get-tuple-element.5), kind=kCustom, calls=%fused_computation.1 | custom fusion | bytes 14696448 | tf_op jit(solution)/shard_map/jit(_take)/gather | solution.py:76
  289.1 43.1 %convolution_convert_fusion = bf16[4096,4096]{1,0:T(8,128)(2,1)} fusion(bf16[4096,896]{1,0:T(8,128)(2,1)} %fusion.4, bf16[4096,896]{1,0:T(8,128)(2,1)} %gather_fusion.1, pred[4096]{0:T(1024)(128)(4,1)S(1)} %compare_and_fusion), kind=kOutput, calls=%fused_computation.7 | convolution fusion | flops 30085218304 | bytes 48238592 | tf_op jit(solution)/shard_map/dot_general | solution.py:78
  332.2 0.0 reduce-scatter.2.cloned.1.call-update
  332.2 0.0 copy-start.1
  332.2 325.7 %reduce-scatter.2.cloned.1.call-done = bf16[512,4096]{1,0:T(8,128)(2,1)} async-done(((bf16[4096,4096]{1,0:T(8,128)(2,1)}), bf16[512,4096]{1,0:T(8,128)(2,1)}) %reduce-scatter.2.cloned.1.call-update) | async-done | bytes 4194320 | tf_op jit(solution)/shard_map/reduce_scatter | solution.py:77
  657.9 9.7 %convert_subtract_fusion = f32[512,4096]{1,0:T(8,128)} fusion(f32[512,4096]{1,0:T(8,128)} %param.15, bf16[512,4096]{1,0:T(8,128)(2,1)} %reduce-scatter.2.cloned.1.call-done), kind=kLoop, calls=%fused_computation.8 | loop fusion | flops 4194304 | bytes 20971520 | tf_op jit(solution)/shard_map/sub | solution.py:83
  667.6 0.0 copy-done.1
  (6 shorter events, 0.1 us)
Async XLA Ops:
  6.5 117.3 %copy-start = (bf16[896,896]{1,0:T(8,128)(2,1)S(1)}, bf16[896,896]{1,0:T(8,128)(2,1)}, u32[]{:S(2)}) copy-start(bf16[896,896]{1,0:T(8,128)(2,1)} %param.14) | copy-start | bytes 4816900
  16.2 37.5 %all-to-all-start = ((s32[4,2,128]{2,1,0:T(2,128)}), s32[4,2,128]{2,1,0:T(2,128)S(1)}, u32[]{:S(2)}, u32[]{:S(2)}) async-start(s32[4,2,128]{2,1,0:T(2,128)} %pad_add_fusion), calls=%async_computation | async-start | bytes 8192 | tf_op jit(solution)/shard_map/all_to_all | solution.py:55
  53.7 8.7 %all-to-all-start.1 = ((f32[4,1,128]{2,1,0:T(1,128)}), f32[4,1,128]{2,1,0:T(1,128)S(1)}, u32[]{:S(2)}, u32[]{:S(2)}) async-start(f32[4,1,128]{2,1,0:T(1,128)} %bitcast.12), calls=%async_computation.1 | async-start | bytes 4096 | tf_op jit(solution)/shard_map/all_to_all | solution.py:56
  57.9 205.9 %all-gather.2.cloned.1.call-start = ((), (), s32[]{:S(2)}) async-start(), calls=%async_computation.3 | async-start | bytes 13762560 | tf_op jit(solution)/shard_map/all_gather | solution.py:75
  151.0 4.1 copy-start.2
  154.9 503.1 %reduce-scatter.2.cloned.1.call-start = ((), (), s32[]{:S(2)}) async-start(), calls=%async_computation.4 | async-start | bytes 37748736 | tf_op jit(solution)/shard_map/reduce_scatter | solution.py:77
  332.2 335.4 %copy-start.1 = (bf16[896,896]{1,0:T(8,128)(2,1)S(1)}, bf16[896,896]{1,0:T(8,128)(2,1)}, u32[]{:S(2)}) copy-start(bf16[896,896]{1,0:T(8,128)(2,1)} %param.14) | copy-start | bytes 4816900
Sparse Core Ops, SparseCore 0:
  155.0 108.7 all-gather.1
  332.4 325.5 reduce-scatter.1
where the time goes:
time: 676 us; the launch traced here: 674 us
  waiting for transfers between devices  439 us (65%)
  other arithmetic  92.6 us (14%)
  local copies, waits for them, and re-layouts  60.7 us (9%)
  matrix products  59.1 us (9%)
  between operations  13.5 us (2%)
  starting transfers between devices  9.62 us (1%)
    reduce_scatter x1, waiting for transfers between devices, per_device(): lax.psum_scatter(jnp.dot(panel_solved.T, solved, preferred_element_type=j...  326 us
    all_gather x1, waiting for transfers between devices, per_device(): gathered = lax.all_gather(local_columns, 'row', axis=1, tiled=True)  109 us
    scatter-add x1, other arithmetic, per_device(): summed = child_update.astype(jnp.float32).at[index_back[:, 0, :].ravel(),...  61.5 us
    dot_general x1, matrix products, per_device(): jnp.dot(panel_solved.T, solved, preferred_element_type=jnp.float32)  43.1 us
    gather x1, local copies, waits for them, and re-layouts, per_device(): panel_solved = jnp.take(gathered, placed, axis=1)  25.3 us
    dot_general x1, matrix products, per_device(): jnp.dot(interior_inverse, coupling, preferred_element_type=jnp.float32)  16.1 us
    scatter x1, local copies, waits for them, and re-layouts, panel_slots(): chosen = jnp.zeros((panel_limit,), jnp.int32).at[picked].set(panel_pores...  15.5 us
  transfers between devices with their start and end apart: 4, of which 3 were waited for; matrix products, arithmetic and copies ran while one was open for 5% of the time, Pallas kernels for 0%

commit v1 on v0

--- a/solution.py
+++ b/solution.py
@@ -2,6 +2,26 @@
 import jax.numpy as jnp
 from jax import lax
 from jax.sharding import PartitionSpec as P
+
+
+def edit_plate_all(u_in, dim_no):
+    v_next = list(u_in.shape[1:])
+    v_next[dim_no] *= u_in.shape[0]
+    return jnp.moveaxis(u_in, 0, dim_no).reshape(v_next)
+
+
+def lead_the_works(x_in, along_axis):
+    arr_next = lax.axis_size(along_axis)
+    fresh, spare = (arr_next, lax.axis_index(along_axis))
+    z, main = (x_in[None], 1)
+    while main < fresh:
+        block_next = lax.ppermute(
+            z, axis_name=along_axis, perm=[(m, m ^ main) for m in range(fresh)]
+        )
+        met_up = spare & main == 0
+        z = jnp.concatenate([jnp.where(met_up, z, block_next), jnp.where(met_up, block_next, z)])
+        main *= 2
+    return z
 
 
 def rank_within(owners, owner_count):
@@ -72,7 +92,8 @@
     )
     chosen, placed = panel_slots(panel_pores, owner_width, row_count, row_index)
     local_columns = jnp.take(solved, chosen, axis=1)
-    gathered = lax.all_gather(local_columns, "row", axis=1, tiled=True)
+    kept_arr = lead_the_works(local_columns, "row")
+    gathered = edit_plate_all(kept_arr, 1)
     panel_solved = jnp.take(gathered, placed, axis=1)
     update = lax.psum_scatter(
         jnp.dot(panel_solved.T, solved, preferred_element_type=jnp.float32).astype(jnp.bfloat16),

time: 676 us -> 762 us (1.13)
  waiting for transfers between devices: 439 us -> 507 us
  other arithmetic: 92.6 us -> 109 us
    ppermute x0 -> x2, waiting for transfers between devices: none -> 177 us  [lead_the_works(): lax.ppermute(z, axis_name=along_axis, perm=[(m, m ^ main) for m in range(...]
    all_gather x1 -> x0, waiting for transfers between devices: 109 us -> none  [per_device(): gathered = lax.all_gather(local_columns, 'row', axis=1, tiled=True)]
    concatenate x0 -> x2, other arithmetic: none -> 8.29 us  [lead_the_works(): jnp.concatenate([jnp.where(met_up, z, block_next), jnp.where(met_up, bloc...]
    select_n x0 -> x2, other arithmetic: none -> 8.13 us  [lead_the_works(): jnp.where(met_up, z, block_next)]
  transfers between devices with their start and end apart: 4 -> 5, of which waited for: 3 -> 4; matrix products, arithmetic and copies ran while one was open for 5% -> 4% of each run, Pallas kernels for 0% -> 0%
where the time goes in v1:
time: 762 us; the launch traced here: 760 us
  waiting for transfers between devices  507 us (67%)
  other arithmetic  109 us (14%)
  local copies, waits for them, and re-layouts  61.7 us (8%)
  matrix products  59.1 us (8%)
  between operations  13.5 us (2%)
  starting transfers between devices  10.3 us (1%)
    reduce_scatter x1, waiting for transfers between devices, per_device(): lax.psum_scatter(jnp.dot(panel_solved.T, solved, preferred_element_type=j...  325 us
    ppermute x2, waiting for transfers between devices, lead_the_works(): lax.ppermute(z, axis_name=along_axis, perm=[(m, m ^ main) for m in range(...  177 us
    scatter-add x1, other arithmetic, per_device(): summed = child_update.astype(jnp.float32).at[index_back[:, 0, :].ravel(),...  61.5 us
    dot_general x1, matrix products, per_device(): jnp.dot(panel_solved.T, solved, preferred_element_type=jnp.float32)  43.1 us
    gather x1, local copies, waits for them, and re-layouts, per_device(): panel_solved = jnp.take(gathered, placed, axis=1)  25.5 us
    dot_general x1, matrix products, per_device(): jnp.dot(interior_inverse, coupling, preferred_element_type=jnp.float32)  16.1 us
    scatter x1, local copies, waits for them, and re-layouts, panel_slots(): chosen = jnp.zeros((panel_limit,), jnp.int32).at[picked].set(panel_pores...  15.5 us
  transfers between devices with their start and end apart: 5, of which 4 were waited for; matrix products, arithmetic and copies ran while one was open for 4% of the time, Pallas kernels for 0%

profile of v1, /device:TPU:0, one launch (start us, length us, event | category | flops | bytes accessed | tf_op | source)
XLA Modules:
  0.0 760.2 jit_solution(14939404080508389294)
XLA Ops:
  6.5 0.0 copy-start
  6.5 0.8 fusion.17
  7.3 1.2 reduce-window.16
  8.6 0.2 slice_reduce_fusion.1
  8.8 0.2 reduce-window.19
  8.9 0.1 add_bitcast_fusion.1
  9.0 0.7 fusion.16
  9.7 0.7 compare_select_fusion.5
  10.4 2.6 scatter_custom_fusion.2
  13.0 2.6 scatter_custom_fusion.1
  15.6 0.6 pad_add_fusion
  16.2 5.2 all-to-all-start
  21.4 0.7 add_select_fusion
  22.1 1.2 reduce-window.14
  23.3 0.2 slice_reduce_fusion
  23.5 0.2 reduce-window.15
  23.7 0.1 add_bitcast_fusion
  23.8 0.1 fusion.10
  23.9 0.7 broadcast_clamp_fusion
  24.7 15.5 %scatter_custom_fusion = s32[1536]{0:T(1024)S(1)} fusion(s32[4096]{0:T(1024)S(1)} %get-tuple-element.10, s32[4096]{0:T(1024)S(1)} %get-tuple-element.11, s32[]{:T(128)} %constant.39.clone.1), kind=kCustom, calls=%fused_computation.60 | custom fusion | bytes 6148 | tf_op jit(solution)/shard_map/scatter | solution.py:44
  40.2 10.3 %convert_element_type.34 = f32[896,4096]{1,0:T(8,128)} convert(bf16[896,4096]{1,0:T(8,128)(2,1)} %param.12) | non-fusion elementwise | flops 3670016 | bytes 22020096 | tf_op jit(solution)/shard_map/convert_element_type | solution.py:85
  50.5 3.2 scatter_custom_fusion.3
  53.7 0.0 all-to-all-done
  53.7 4.2 all-to-all-start.1
  57.9 0.0 reduce-scatter.2.cloned.1.call-start
  57.9 4.5 all-to-all-done.1
  62.4 61.5 %scatter_fusion = f32[896,4096]{1,0:T(8,128)} fusion(f32[896,4096]{1,0:T(8,128)} %convert_element_type.34, s32[512]{0:T(512)S(1)} %bitcast.75, f32[512]{0:T(512)S(1)} %bitcast.78), kind=kCustom, calls=%fused_computation.6 | custom fusion | flops 512 | bytes 10240 | tf_op jit(solution)/shard_map/scatter-add | solution.py:87
  123.8 0.0 copy-done
  123.8 16.1 %fusion.4 = bf16[4096,896]{1,0:T(8,128)(2,1)} fusion(bf16[896,896]{1,0:T(8,128)(2,1)S(1)} %copy-done, f32[896,4096]{1,0:T(8,128)} %scatter_fusion), kind=kOutput, calls=%fused_computation.14 | convolution fusion | flops 6584008704 | bytes 23625728 | tf_op jit(solution)/shard_map/dot_general | solution.py:90
  139.9 11.1 %gather_fusion = bf16[1536,896]{1,0:T(8,128)(2,1)} fusion(bf16[896,4096]{0,1:T(8,128)(2,1)} %bitcast.74, s32[2048]{0:T(1024)S(1)} %pad_clamp_fusion), kind=kCustom, calls=%fused_computation | custom fusion | bytes 5511168 | tf_op jit(solution)/shard_map/jit(_take)/gather | solution.py:94
  151.0 3.7 bitcast_select_fusion
  154.7 0.6 collective-permute-start
  155.3 59.4 %collective-permute-done = bf16[1,896,1536]{1,2,0:T(8,128)(2,1)} collective-permute-done((bf16[1,896,1536]{1,2,0:T(8,128)(2,1)}, bf16[1,896,1536]{1,2,0:T(8,128)(2,1)}, u32[]{:S(2)}, u32[]{:S(2)}) %collective-permute-start) | collective-permute-done | bytes 2752544 | tf_op jit(solution)/shard_map/ppermute | solution.py:18
  214.7 3.2 broadcast_select_fusion.3
  217.8 0.0 copy-start.2
  217.9 0.0 copy-start.4
  217.9 3.3 pad_maximum_fusion.1
  221.2 0.8 copy-done.3
  222.0 0.3 collective-permute-start.1
  222.3 117.7 %collective-permute-done.1 = bf16[2,896,1536]{1,2,0:T(8,128)(2,1)} collective-permute-done((bf16[2,896,1536]{1,2,0:T(8,128)(2,1)}, bf16[2,896,1536]{1,2,0:T(8,128)(2,1)}, u32[]{:S(2)}, u32[]{:S(2)}) %collective-permute-start.1) | collective-permute-done | bytes 5505056 | tf_op jit(solution)/shard_map/ppermute | solution.py:18
  340.0 5.0 broadcast_select_fusion.1
  345.0 5.0 pad_maximum_fusion
  350.0 25.5 %gather_fusion.1 = bf16[4096,896]{1,0:T(8,128)(2,1)} fusion(bf16[896,6144]{0,1:T(8,128)(2,1)} %bitcast.73, s32[4096]{0:T(1024)S(1)} %get-tuple-element.9), kind=kCustom, calls=%fused_computation.1 | custom fusion | bytes 14696448 | tf_op jit(solution)/shard_map/jit(_take)/gather | solution.py:97
  375.5 43.1 %convolution_convert_fusion = bf16[4096,4096]{1,0:T(8,128)(2,1)} fusion(bf16[4096,896]{1,0:T(8,128)(2,1)} %fusion.4, bf16[4096,896]{1,0:T(8,128)(2,1)} %gather_fusion.1, pred[4096]{0:T(1024)(128)(4,1)S(1)} %compare_and_fusion), kind=kOutput, calls=%fused_computation.7 | convolution fusion | flops 30085218304 | bytes 48238592 | tf_op jit(solution)/shard_map/dot_general | solution.py:99
  418.6 0.0 reduce-scatter.2.cloned.1.call-update
  418.6 0.0 copy-start.1
  418.6 325.0 %reduce-scatter.2.cloned.1.call-done = bf16[512,4096]{1,0:T(8,128)(2,1)} async-done(((bf16[4096,4096]{1,0:T(8,128)(2,1)}), bf16[512,4096]{1,0:T(8,128)(2,1)}) %reduce-scatter.2.cloned.1.call-update) | async-done | bytes 4194320 | tf_op jit(solution)/shard_map/reduce_scatter | solution.py:98
  743.6 9.7 %convert_subtract_fusion = f32[512,4096]{1,0:T(8,128)} fusion(f32[512,4096]{1,0:T(8,128)} %param.15, bf16[512,4096]{1,0:T(8,128)(2,1)} %reduce-scatter.2.cloned.1.call-done), kind=kLoop, calls=%fused_computation.9 | loop fusion | flops 4194304 | bytes 20971520 | tf_op jit(solution)/shard_map/sub | solution.py:104
  (10 shorter events, 0.1 us)
Async XLA Ops:
  6.5 117.3 %copy-start = (bf16[896,896]{1,0:T(8,128)(2,1)S(1)}, bf16[896,896]{1,0:T(8,128)(2,1)}, u32[]{:S(2)}) copy-start(bf16[896,896]{1,0:T(8,128)(2,1)} %param.14) | copy-start | bytes 4816900
  16.2 37.5 %all-to-all-start = ((s32[4,2,128]{2,1,0:T(2,128)}), s32[4,2,128]{2,1,0:T(2,128)S(1)}, u32[]{:S(2)}, u32[]{:S(2)}) async-start(s32[4,2,128]{2,1,0:T(2,128)} %pad_add_fusion), calls=%async_computation | async-start | bytes 8192 | tf_op jit(solution)/shard_map/all_to_all | solution.py:75
  53.7 8.7 %all-to-all-start.1 = ((f32[4,1,128]{2,1,0:T(1,128)}), f32[4,1,128]{2,1,0:T(1,128)S(1)}, u32[]{:S(2)}, u32[]{:S(2)}) async-start(f32[4,1,128]{2,1,0:T(1,128)} %bitcast.12), calls=%async_computation.1 | async-start | bytes 4096 | tf_op jit(solution)/shard_map/all_to_all | solution.py:76
  57.9 685.8 %reduce-scatter.2.cloned.1.call-start = ((), (), s32[]{:S(2)}) async-start(), calls=%async_computation.3 | async-start | bytes 37748736 | tf_op jit(solution)/shard_map/reduce_scatter | solution.py:98
  154.7 60.0 %collective-permute-start = (bf16[1,896,1536]{1,2,0:T(8,128)(2,1)}, bf16[1,896,1536]{1,2,0:T(8,128)(2,1)}, u32[]{:S(2)}, u32[]{:S(2)}) collective-permute-start(bf16[1,896,1536]{1,2,0:T(8,128)(2,1)} %bitcast_select_fusion), channel_id=1, source_target_pairs={{0,8},{8,0},{16,24},{24,16},{1,9},{9,1},{17,25},{25,17},{2,10},{10... | collective-permute-start | bytes 8257544 | tf_op jit(solution)/shard_map/ppermute | solution.py:18
  217.8 3.4 copy-start.2
  217.9 4.1 copy-start.3
  217.9 4.5 copy-start.4
  222.0 118.0 %collective-permute-start.1 = (bf16[2,896,1536]{1,2,0:T(8,128)(2,1)}, bf16[2,896,1536]{1,2,0:T(8,128)(2,1)}, u32[]{:S(2)}, u32[]{:S(2)}) collective-permute-start(bf16[2,896,1536]{1,2,0:T(8,128)(2,1)} %pad_maximum_fusion.1), channel_id=1, source_target_pairs={{0,16},{8,24},{16,0},{24,8},{1,17},{9,25},{17,1},{25,9},{2,18},{10... | collective-permute-start | bytes 16515080 | tf_op jit(solution)/shard_map/ppermute | solution.py:18
  418.6 334.7 %copy-start.1 = (bf16[896,896]{1,0:T(8,128)(2,1)S(1)}, bf16[896,896]{1,0:T(8,128)(2,1)}, u32[]{:S(2)}) copy-start(bf16[896,896]{1,0:T(8,128)(2,1)} %param.14) | copy-start | bytes 4816900
Sparse Core Ops, SparseCore 0:
  418.7 324.8 reduce-scatter.1
